TPU v7x, 32 devices: a whole 2x2x4 slice. The times are simulated.
32 devices in a mesh: dp: 4 (over y, x), ctx: 4 (over z), head: 2 (over core).
Axes of the slice: x: 2, y: 2, z: 4, core: 2. Of those that a mesh axis runs over, the one named last changes fastest.
Arguments:
- inputs: bfloat16 [4, 512, 2048], P('dp', 'ctx', 'head'), may hold values from -1.5 to 1.5
- dt_raw: float32 [4, 512, 32], P('dp', 'ctx', 'head'), may hold values from -4 to 4
- dt_bias: float32 [32], P('head'), may hold values from -1 to 1
- a_log: float32 [32], P('head'), may hold values from -30 to -2.8
- b_in: bfloat16 [4, 512, 128], P('dp', 'ctx'), may hold values from -0.13183594 to 0.13183594
- c_in: bfloat16 [4, 512, 128], P('dp', 'ctx'), may hold values from -0.13183594 to 0.13183594
- skip_gain: float32 [32], P('head'), may hold values from 0.5 to 1.5
- grad_out: bfloat16 [4, 512, 2048], P('dp', 'ctx', 'head'), may hold values from -1.5 to 1.5
- doc_lengths: int32 [4, 4], P('dp'), may hold values from 1 to 256, 512 in all within a row
Outputs:
- grad_inputs: bfloat16 [4, 512, 2048], P('dp', 'ctx', 'head')
- grad_dt_raw: float32 [4, 512, 32], P('dp', 'ctx', 'head')
- grad_b: float32 [4, 512, 128], P('dp', 'ctx')
- grad_c: float32 [4, 512, 128], P('dp', 'ctx')
- grad_a_log: float32 [32], P('head')
- grad_dt_bias: float32 [32], P('head')
- grad_skip: float32 [32], P('head')
Inputs may be any that keep to these rules, and one draw needn't show every extreme that they name: `doc_lengths`: each row lists 4 document lengths laid end to end from the sequence's first position; they sum to 512, and the longest is exactly half of 512.
All inputs are finite; a program needn't handle non-finite values.
Results may differ from a plain program's by a relative error of at most 0.007.
Values sent between devices are 32-bit elements; how exact they have to be, the bound alone decides.
No kernel may reach another device: no remote copies, remote signals or barrier semaphores. Data moves between devices by JAX's collectives and lax.ppermute only.
A program may use at most 64 MiB of HBM per device.

v0:
```python
import jax
import jax.numpy as jnp
from jax import lax
from jax.sharding import PartitionSpec as P

SPAN = 128


def from_behind(array, axis, by):
    count = lax.axis_size(axis)
    pairs = [(i, i + by) for i in range(count) if 0 <= i + by < count]
    return lax.ppermute(array, axis, pairs)


def reverse_cumsum(values, along_axis):
    return jnp.flip(jnp.cumsum(jnp.flip(values, along_axis), axis=along_axis), along_axis)


def doc_index(positions, starts):
    return jnp.sum((starts[None, :] <= positions[:, None]).astype(jnp.int32), axis=1)


def vector_factors(decay_block, segment_block, previous_block):
    cumulative = jnp.cumsum(decay_block, axis=0)
    last_segment = segment_block[-1]
    mask_in = (segment_block == previous_block).astype(jnp.float32)
    mask_out = (segment_block == last_segment).astype(jnp.float32)
    factor_in = mask_in[:, None] * jnp.exp(cumulative)
    factor_out = mask_out[:, None] * jnp.exp(cumulative[-1][None, :] - cumulative)
    span_total = (last_segment == previous_block).astype(jnp.float32) * jnp.exp(cumulative[-1])
    return (cumulative, mask_in, mask_out, factor_in, factor_out, span_total)


def pair_factor(cumulative, segment_block):
    local_pos = jnp.arange(segment_block.shape[0], dtype=jnp.int32)
    allowed = (local_pos[:, None] >= local_pos[None, :]) & (
        segment_block[:, None] == segment_block[None, :]
    )
    spread = cumulative.T[:, :, None] - cumulative.T[:, None, :]
    return jnp.where(allowed[None], jnp.exp(jnp.where(allowed[None], spread, 0.0)), 0.0)


def first_pass(
    inputs_block,
    grads_block,
    b_block,
    c_block,
    step_block,
    decay_block,
    segment_block,
    previous_block,
):
    cumulative, mask_in, mask_out, factor_in, factor_out, span_total = vector_factors(
        decay_block, segment_block, previous_block
    )
    scaled_in = (inputs_block * (factor_out * step_block)[:, :, None]).astype(jnp.bfloat16)
    scaled_grad = (grads_block * factor_in[:, :, None]).astype(jnp.bfloat16)
    state_part = jnp.einsum("shp,sn->hpn", scaled_in, b_block, preferred_element_type=jnp.float32)
    grad_part = jnp.einsum("uhp,un->hpn", scaled_grad, c_block, preferred_element_type=jnp.float32)
    return (span_total, state_part, grad_part)


def span_grads(
    inputs_block,
    grads_block,
    b_block,
    c_block,
    step_block,
    decay_block,
    segment_block,
    previous_block,
    preact_block,
    state_in,
    state_grad,
    decay_rate,
    skip_gain,
):
    cumulative, mask_in, mask_out, factor_in, factor_out, span_total = vector_factors(
        decay_block, segment_block, previous_block
    )
    pair_decay = pair_factor(cumulative, segment_block)
    scores = jnp.einsum("un,sn->us", c_block, b_block, preferred_element_type=jnp.float32)
    cross_term = jnp.einsum(
        "uhp,shp->hus", grads_block, inputs_block, preferred_element_type=jnp.float32
    )
    masked = (pair_decay * scores[None]).astype(jnp.bfloat16)
    weighted = pair_decay * cross_term * step_block.T[:, None, :]
    summed = jnp.sum(weighted, axis=0).astype(jnp.bfloat16)
    products = weighted * scores[None]
    change = jnp.sum(products, axis=2) - jnp.sum(products, axis=1)
    first_term = reverse_cumsum(change, 1).T
    h_low = state_in.astype(jnp.bfloat16)
    e_low = state_grad.astype(jnp.bfloat16)
    along_b = jnp.einsum("tn,hpn->thp", b_block, e_low, preferred_element_type=jnp.float32)
    grad_b_prod = (
        jnp.einsum("hut,uhp->thp", masked, grads_block, preferred_element_type=jnp.float32)
        + factor_out[:, :, None] * along_b
    )
    grad_x = (step_block[:, :, None] * grad_b_prod + skip_gain[None, :, None] * grads_block).astype(
        jnp.bfloat16
    )
    x_state = jnp.einsum("thp,hpn->thn", inputs_block, e_low, preferred_element_type=jnp.float32)
    y_state = jnp.einsum("uhp,hpn->uhn", grads_block, h_low, preferred_element_type=jnp.float32)
    grad_b = jnp.einsum("us,un->sn", summed, c_block, preferred_element_type=jnp.float32) + jnp.sum(
        (step_block * factor_out)[:, :, None] * x_state, axis=1
    )
    grad_c = jnp.einsum("us,sn->un", summed, b_block, preferred_element_type=jnp.float32) + jnp.sum(
        factor_in[:, :, None] * y_state, axis=1
    )
    z_term = jnp.sum(y_state * c_block[:, None, :], axis=2)
    w_term = step_block * jnp.sum(x_state * b_block[:, None, :], axis=2)
    second_term = mask_in[:, None] * reverse_cumsum(factor_in * z_term, 0)
    carried = factor_out * w_term
    third_term = mask_out[:, None] * (jnp.cumsum(carried, axis=0) - carried)
    fourth_term = factor_out * factor_in * jnp.sum(state_grad * state_in, axis=(1, 2))[None, :]
    decay_grad = first_term + second_term + third_term + fourth_term
    x_dot_g = jnp.sum(inputs_block * grad_b_prod, axis=2)
    grad_dt = (x_dot_g + decay_rate[None, :] * decay_grad) * jax.nn.sigmoid(preact_block)
    grad_alog = jnp.sum(decay_grad * step_block, axis=0) * decay_rate
    grad_bias = jnp.sum(grad_dt, axis=0)
    grad_skip = jnp.einsum(
        "thp,thp->h", grads_block, inputs_block, preferred_element_type=jnp.float32
    )
    return (grad_x, grad_dt, grad_b, grad_c, grad_alog, grad_bias, grad_skip)


def local_link(running, pieces):
    decay_gain, held_state = running
    span_total, span_part = pieces
    return ((decay_gain * span_total, span_total[:, None, None] * held_state + span_part), running)


def link_maps(earlier, later):
    return (earlier[0] * later[0], later[0][:, None, None] * earlier[1] + later[1])


def doubling(element, reverse):
    axis_count = lax.axis_size("ctx")
    own_index = lax.axis_index("ctx")
    distances = [1] + [2**power for power in range((axis_count - 1).bit_length())]
    running = element
    for section_num, distance in enumerate(distances):
        shift_by = -distance if reverse else distance
        received = from_behind((running[0], running[1]), "ctx", shift_by)
        source = own_index - shift_by
        present = (source >= 0) & (source < axis_count)
        fixed = (jnp.where(present, received[0], 1.0), received[1])
        if section_num == 0:
            running = fixed
        else:
            running = link_maps(fixed, running)
    return running


def local(inputs, dt_raw, dt_bias, a_log, b_in, c_in, skip_gain, grad_out, doc_lengths):
    token_count = inputs.shape[1]
    head_count = dt_bias.shape[0]
    head_width = inputs.shape[2] // head_count
    state_size = b_in.shape[2]
    span_count = token_count // SPAN
    preact = dt_raw[0] + dt_bias[None, :]
    step_size = jax.nn.softplus(preact)
    decay_rate = -jnp.exp(a_log)
    log_decay = step_size * decay_rate[None, :]
    lengths = doc_lengths[0]
    starts = jnp.cumsum(lengths) - lengths
    positions = lax.axis_index("ctx") * token_count + jnp.arange(token_count, dtype=jnp.int32)
    segment = doc_index(positions, starts)
    previous = doc_index(positions[::SPAN] - 1, starts)
    shaped = (
        inputs[0].reshape(span_count, SPAN, head_count, head_width),
        grad_out[0].reshape(span_count, SPAN, head_count, head_width),
        b_in[0].reshape(span_count, SPAN, state_size),
        c_in[0].reshape(span_count, SPAN, state_size),
        step_size.reshape(span_count, SPAN, head_count),
        log_decay.reshape(span_count, SPAN, head_count),
        segment.reshape(span_count, SPAN),
        previous,
    )
    totals, state_parts, grad_parts = jax.vmap(first_pass)(*shaped)
    start_maps = (
        jnp.ones((head_count,), jnp.float32),
        jnp.zeros((head_count, head_width, state_size), jnp.float32),
    )
    forward_map, (gain_before, local_entry) = lax.scan(
        local_link, start_maps, (totals, state_parts)
    )
    backward_map, (gain_after, local_leave) = lax.scan(
        local_link, start_maps, (totals, grad_parts), reverse=True
    )
    entry_state = doubling(forward_map, False)[1]
    leave_state = doubling(backward_map, True)[1]
    entering = gain_before[:, :, None, None] * entry_state[None] + local_entry
    leaving = gain_after[:, :, None, None] * leave_state[None] + local_leave
    mapped = jax.vmap(span_grads, in_axes=(0, 0, 0, 0, 0, 0, 0, 0, 0, 0, 0, None, None))
    grad_x, grad_dt, grad_b, grad_c, grad_alog, grad_bias, grad_skip = mapped(
        *shaped,
        preact.reshape(span_count, SPAN, head_count),
        entering,
        leaving,
        decay_rate,
        skip_gain
    )
    b_total, c_total = lax.psum(
        (grad_b.reshape(token_count, state_size), grad_c.reshape(token_count, state_size)), "head"
    )
    alog_total, bias_total, skip_total = lax.psum(
        (jnp.sum(grad_alog, axis=0), jnp.sum(grad_bias, axis=0), jnp.sum(grad_skip, axis=0)),
        ("dp", "ctx"),
    )
    return (
        grad_x.reshape(1, token_count, head_count * head_width),
        grad_dt,
        b_total[None],
        c_total[None],
        alog_total,
        bias_total,
        skip_total,
    )


def solution(mesh):
    placed = (
        P("dp", "ctx", "head"),
        P("dp", "ctx", "head"),
        P("head"),
        P("head"),
        P("dp", "ctx", None),
        P("dp", "ctx", None),
        P("head"),
        P("dp", "ctx", "head"),
        P("dp", None),
    )
    return jax.shard_map(
        local,
        mesh=mesh,
        in_specs=placed,
        out_specs=(
            P("dp", "ctx", "head"),
            P("dp", "ctx", "head"),
            P("dp", "ctx", None),
            P("dp", "ctx", None),
            P("head"),
            P("head"),
            P("head"),
        ),
        check_vma=False,
    )
```

profile of v0, /device:TPU:0, one launch (start us, length us, event | category | flops | bytes accessed | tf_op | source)
XLA Modules:
  0.0 140.7 jit_solution(209060816925791621)
XLA Ops:
  7.3 0.8 reduce-window_clone.1
  8.1 1.3 fusion.37
  10.1 0.8 copy.101
  13.7 1.3 collective-permute-start
  15.0 5.6 %collective-permute-start.5 = (f32[16]{0:T(128)S(1)}, f32[16]{0:T(128)S(1)}, u32[]{:S(2)}, u32[]{:S(2)}) collective-permute-start(f32[16]{0:T(128)S(1)} %get-tuple-element.102), channel_id=1, source_target_pairs={{0,2},{2,4},{4,6},{1,3},{3,5},{5,7},{8,10},{10,12},{12,14},{9,11},... | collective-permute-start | bytes 200 | tf_op jit(solution)/shard_map/ppermute | solution.py:12
  20.7 1.3 compare_convert_fusion
  23.3 1.4 %collective-permute-start.2 = (f32[16,64,128]{2,1,0:T(8,128)S(1)}, f32[16,64,128]{2,1,0:T(8,128)S(1)}, u32[]{:S(2)}, u32[]{:S(2)}) collective-permute-start(f32[16,64,128]{2,1,0:T(8,128)S(1)} %convolution_add_fusion.1), channel_id=1, source_target_pairs={{2,0},{4,2},{6,4},{3,1},{5,3},{7,5},{10,8},{12,10},{14,12},{11,9},... | collective-permute-start | bytes 1572872 | tf_op jit(solution)/shard_map/ppermute | solution.py:12
  26.0 4.6 %collective-permute-start.7 = (f32[16,64,128]{2,1,0:T(8,128)S(1)}, f32[16,64,128]{2,1,0:T(8,128)S(1)}, u32[]{:S(2)}, u32[]{:S(2)}) collective-permute-start(f32[16,64,128]{2,1,0:T(8,128)S(1)} %convolution_add_fusion), channel_id=1, source_target_pairs={{0,2},{2,4},{4,6},{1,3},{3,5},{5,7},{8,10},{10,12},{12,14},{9,11},... | collective-permute-start | bytes 1572872 | tf_op jit(solution)/shard_map/ppermute | solution.py:12
  31.6 0.9 multiply_reduce_fusion.4
  32.6 6.1 %collective-permute-done.2 = f32[16,64,128]{2,1,0:T(8,128)S(1)} collective-permute-done((f32[16,64,128]{2,1,0:T(8,128)S(1)}, f32[16,64,128]{2,1,0:T(8,128)S(1)}, u32[]{:S(2)}, u32[]{:S(2)}) %collective-permute-start.2) | collective-permute-done | bytes 524320 | tf_op jit(solution)/shard_map/ppermute | solution.py:12
  38.7 1.3 collective-permute-start.3
  41.2 4.6 %collective-permute-start.8 = (f32[16,64,128]{2,1,0:T(8,128)S(1)}, f32[16,64,128]{2,1,0:T(8,128)S(1)}, u32[]{:S(2)}, u32[]{:S(2)}) collective-permute-start(f32[16,64,128]{2,1,0:T(8,128)S(1)} %collective-permute-done.7), channel_id=1, source_target_pairs={{0,2},{2,4},{4,6},{1,3},{3,5},{5,7},{8,10},{10,12},{12,14},{9,11},... | collective-permute-start | bytes 1572872 | tf_op jit(solution)/shard_map/ppermute | solution.py:12
  45.8 7.3 %collective-permute-done.3 = f32[16,64,128]{2,1,0:T(8,128)} collective-permute-done((f32[16,64,128]{2,1,0:T(8,128)S(1)}, f32[16,64,128]{2,1,0:T(8,128)}, u32[]{:S(2)}, u32[]{:S(2)}) %collective-permute-start.3) | collective-permute-done | bytes 524320 | tf_op jit(solution)/shard_map/ppermute | solution.py:12
  53.2 1.2 multiply_add_fusion.3
  54.3 1.3 collective-permute-start.4
  55.8 5.5 %collective-permute-start.9 = (f32[16,64,128]{2,1,0:T(8,128)S(1)}, f32[16,64,128]{2,1,0:T(8,128)S(1)}, u32[]{:S(2)}, u32[]{:S(2)}) collective-permute-start(f32[16,64,128]{2,1,0:T(8,128)S(1)} %multiply_add_fusion.1), channel_id=1, source_target_pairs={{0,4},{2,6},{1,5},{3,7},{8,12},{10,14},{9,13},{11,15},{16,20},{18,... | collective-permute-start | bytes 1572872 | tf_op jit(solution)/shard_map/ppermute | solution.py:12
  61.5 3.9 %collective-permute-start.6 = (f32[16]{0:T(128)S(1)}, f32[16]{0:T(128)S(1)}, u32[]{:S(2)}, u32[]{:S(2)}) collective-permute-start(f32[16]{0:T(128)S(1)} %broadcast_select_fusion.1), channel_id=1, source_target_pairs={{0,2},{2,4},{4,6},{1,3},{3,5},{5,7},{8,10},{10,12},{12,14},{9,11},... | collective-permute-start | bytes 200 | tf_op jit(solution)/shard_map/ppermute | solution.py:12
  65.4 1.3 collective-permute-start.1
  66.7 3.5 %collective-permute-done.6 = f32[16]{0:T(128)S(1)} collective-permute-done((f32[16]{0:T(128)S(1)}, f32[16]{0:T(128)S(1)}, u32[]{:S(2)}, u32[]{:S(2)}) %collective-permute-start.6) | collective-permute-done | bytes 96 | tf_op jit(solution)/shard_map/ppermute | solution.py:12
  70.9 9.1 %collective-permute-done.4 = f32[16,64,128]{2,1,0:T(8,128)S(1)} collective-permute-done((f32[16,64,128]{2,1,0:T(8,128)S(1)}, f32[16,64,128]{2,1,0:T(8,128)S(1)}, u32[]{:S(2)}, u32[]{:S(2)}) %collective-permute-start.4) | collective-permute-done | bytes 524320 | tf_op jit(solution)/shard_map/ppermute | solution.py:12
  84.4 0.8 fusion.5
  85.9 0.8 copy.120
  87.4 44.3 %all-reduce = (f32[16]{0:T(128)}, f32[16]{0:T(128)}, f32[16]{0:T(128)}) all-reduce(f32[16]{0:T(128)S(1)} %fusion.39, f32[16]{0:T(128)S(1)} %get-tuple-element.96, f32[16]{0:T(128)S(1)} %fusion.6), channel_id=1, replica_groups=mesh['dp'=4,'ctx'=4,'head'=2] {'dp','ctx'}, use_global_device_ids=true, to_apply=%region_19.20 | all-reduce | flops 48 | bytes 384 | tf_op jit(solution)/shard_map/psum | solution.py:207
  131.7 1.5 %copy.134 = f32[1,128,128]{2,1,0:T(8,128)} copy(f32[1,128,128]{2,1,0:T(8,128)} %get-tuple-element.119) | data formatting | bytes 131072
  (86 shorter events, 14.4 us)
Async XLA Ops:
  7.2 14.8 %copy-start.2 = (bf16[1,128,1024]{2,1,0:T(8,128)(2,1)S(1)}, bf16[1,128,1024]{2,1,0:T(8,128)(2,1)}, u32[]{:S(2)}) copy-start(bf16[1,128,1024]{2,1,0:T(8,128)(2,1)} %param.16) | copy-start | bytes 786436
  7.2 124.5 %all-reduce.4.cloned.1.call-start = ((), (), s32[]{:S(2)}) async-start(), calls=%async_computation | async-start | bytes 262144 | tf_op jit(solution)/shard_map/psum | solution.py:204
  13.7 32.1 %collective-permute-start = (f32[16]{0:T(128)S(1)}, f32[16]{0:T(128)S(1)}, u32[]{:S(2)}, u32[]{:S(2)}) collective-permute-start(f32[16]{0:T(128)S(1)} %get-tuple-element.102), channel_id=1, source_target_pairs={{2,0},{4,2},{6,4},{3,1},{5,3},{7,5},{10,8},{12,10},{14,12},{11,9},... | collective-permute-start | bytes 200 | tf_op jit(solution)/shard_map/ppermute | solution.py:12
  15.0 30.8 %collective-permute-start.5 = (f32[16]{0:T(128)S(1)}, f32[16]{0:T(128)S(1)}, u32[]{:S(2)}, u32[]{:S(2)}) collective-permute-start(f32[16]{0:T(128)S(1)} %get-tuple-element.102), channel_id=1, source_target_pairs={{0,2},{2,4},{4,6},{1,3},{3,5},{5,7},{8,10},{10,12},{12,14},{9,11},... | collective-permute-start | bytes 200 | tf_op jit(solution)/shard_map/ppermute | solution.py:12
  22.3 0.8 copy-start.1
  23.0 1.7 %copy-start.6 = (f32[16]{0:T(128)S(1)}, f32[16]{0:T(128)}, u32[]{:S(2)}) copy-start(f32[16]{0:T(128)} %param.11) | copy-start | bytes 196
  23.2 1.6 %copy-start.3 = (bf16[1,128,1024]{2,1,0:T(8,128)(2,1)S(1)}, bf16[1,128,1024]{2,1,0:T(8,128)(2,1)}, u32[]{:S(2)}) copy-start(bf16[1,128,1024]{2,1,0:T(8,128)(2,1)} %param.9) | copy-start | bytes 786436
  23.3 15.4 %collective-permute-start.2 = (f32[16,64,128]{2,1,0:T(8,128)S(1)}, f32[16,64,128]{2,1,0:T(8,128)S(1)}, u32[]{:S(2)}, u32[]{:S(2)}) collective-permute-start(f32[16,64,128]{2,1,0:T(8,128)S(1)} %convolution_add_fusion.1), channel_id=1, source_target_pairs={{2,0},{4,2},{6,4},{3,1},{5,3},{7,5},{10,8},{12,10},{14,12},{11,9},... | collective-permute-start | bytes 1572872 | tf_op jit(solution)/shard_map/ppermute | solution.py:12
  25.0 0.8 copy-start
  26.0 15.2 %collective-permute-start.7 = (f32[16,64,128]{2,1,0:T(8,128)S(1)}, f32[16,64,128]{2,1,0:T(8,128)S(1)}, u32[]{:S(2)}, u32[]{:S(2)}) collective-permute-start(f32[16,64,128]{2,1,0:T(8,128)S(1)} %convolution_add_fusion), channel_id=1, source_target_pairs={{0,2},{2,4},{4,6},{1,3},{3,5},{5,7},{8,10},{10,12},{12,14},{9,11},... | collective-permute-start | bytes 1572872 | tf_op jit(solution)/shard_map/ppermute | solution.py:12
  30.7 0.7 copy-start.5
  38.7 14.5 %collective-permute-start.3 = (f32[16,64,128]{2,1,0:T(8,128)S(1)}, f32[16,64,128]{2,1,0:T(8,128)}, u32[]{:S(2)}, u32[]{:S(2)}) collective-permute-start(f32[16,64,128]{2,1,0:T(8,128)S(1)} %collective-permute-done.2), channel_id=1, source_target_pairs={{2,0},{4,2},{6,4},{3,1},{5,3},{7,5},{10,8},{12,10},{14,12},{11,9},... | collective-permute-start | bytes 1572872 | tf_op jit(solution)/shard_map/ppermute | solution.py:12
  41.2 14.4 %collective-permute-start.8 = (f32[16,64,128]{2,1,0:T(8,128)S(1)}, f32[16,64,128]{2,1,0:T(8,128)S(1)}, u32[]{:S(2)}, u32[]{:S(2)}) collective-permute-start(f32[16,64,128]{2,1,0:T(8,128)S(1)} %collective-permute-done.7), channel_id=1, source_target_pairs={{0,2},{2,4},{4,6},{1,3},{3,5},{5,7},{8,10},{10,12},{12,14},{9,11},... | collective-permute-start | bytes 1572872 | tf_op jit(solution)/shard_map/ppermute | solution.py:12
  54.3 25.7 %collective-permute-start.4 = (f32[16,64,128]{2,1,0:T(8,128)S(1)}, f32[16,64,128]{2,1,0:T(8,128)S(1)}, u32[]{:S(2)}, u32[]{:S(2)}) collective-permute-start(f32[16,64,128]{2,1,0:T(8,128)S(1)} %multiply_add_fusion.3), channel_id=1, source_target_pairs={{4,0},{6,2},{5,1},{7,3},{12,8},{14,10},{13,9},{15,11},{20,16},{22,... | collective-permute-start | bytes 1572872 | tf_op jit(solution)/shard_map/ppermute | solution.py:12
  55.8 24.3 %collective-permute-start.9 = (f32[16,64,128]{2,1,0:T(8,128)S(1)}, f32[16,64,128]{2,1,0:T(8,128)S(1)}, u32[]{:S(2)}, u32[]{:S(2)}) collective-permute-start(f32[16,64,128]{2,1,0:T(8,128)S(1)} %multiply_add_fusion.1), channel_id=1, source_target_pairs={{0,4},{2,6},{1,5},{3,7},{8,12},{10,14},{9,13},{11,15},{16,20},{18,... | collective-permute-start | bytes 1572872 | tf_op jit(solution)/shard_map/ppermute | solution.py:12
  61.5 8.7 %collective-permute-start.6 = (f32[16]{0:T(128)S(1)}, f32[16]{0:T(128)S(1)}, u32[]{:S(2)}, u32[]{:S(2)}) collective-permute-start(f32[16]{0:T(128)S(1)} %broadcast_select_fusion.1), channel_id=1, source_target_pairs={{0,2},{2,4},{4,6},{1,3},{3,5},{5,7},{8,10},{10,12},{12,14},{9,11},... | collective-permute-start | bytes 200 | tf_op jit(solution)/shard_map/ppermute | solution.py:12
  65.4 5.5 %collective-permute-start.1 = (f32[16]{0:T(128)S(1)}, f32[16]{0:T(128)S(1)}, u32[]{:S(2)}, u32[]{:S(2)}) collective-permute-start(f32[16]{0:T(128)S(1)} %broadcast_select_fusion.3), channel_id=1, source_target_pairs={{2,0},{4,2},{6,4},{3,1},{5,3},{7,5},{10,8},{12,10},{14,12},{11,9},... | collective-permute-start | bytes 200 | tf_op jit(solution)/shard_map/ppermute | solution.py:12
  82.1 0.7 copy-start.7
  86.7 0.7 copy-start.8
  131.7 1.5 %copy-start.4 = (f32[1,128,128]{2,1,0:T(8,128)S(1)}, f32[1,128,128]{2,1,0:T(8,128)}, u32[]{:S(2)}) copy-start(f32[1,128,128]{2,1,0:T(8,128)} %get-tuple-element.120) | copy-start | bytes 196612
Sparse Core Ops, SparseCore 0:
  86.9 20.8 all-reduce.3
where the time goes:
time: 141 us
  blocking collectives  44.3 us (31%)
  starting transfers between devices  30.8 us (22%)
  waiting for transfers between devices  26.8 us (19%)
  between operations  15.8 us (11%)
  local copies, waits for them, and re-layouts  9.75 us (7%)
  other arithmetic  8.3 us (6%)
  matrix products  4.97 us (4%)
    psum x1, blocking collectives, local(): lax.psum((jnp.sum(grad_alog, axis=0), jnp.sum(grad_bias, axis=0), jnp.sum...  44.3 us
    ppermute x10, starting transfers between devices, from_behind(): return lax.ppermute(array, axis, pairs)  30.8 us
    ppermute x10, waiting for transfers between devices, from_behind(): return lax.ppermute(array, axis, pairs)  26.8 us
    unnamed x25, local copies, waits for them, and re-layouts  8.06 us
  transfers between devices with their start and end apart: 11, of which 5 were waited for; matrix products, arithmetic and copies ran while one was open for 5% of the time, Pallas kernels for 0%

commit v1 on v0

--- a/solution.py
+++ b/solution.py
@@ -4,6 +4,12 @@
 from jax.sharding import PartitionSpec as P
 
 SPAN = 128
+
+
+def load_islands(q_in):
+    s_next = lax.psum(q_in, "ctx")
+    x_next = lax.psum(s_next, "dp")
+    return x_next
 
 
 def from_behind(array, axis, by):
@@ -204,9 +210,8 @@
     b_total, c_total = lax.psum(
         (grad_b.reshape(token_count, state_size), grad_c.reshape(token_count, state_size)), "head"
     )
-    alog_total, bias_total, skip_total = lax.psum(
-        (jnp.sum(grad_alog, axis=0), jnp.sum(grad_bias, axis=0), jnp.sum(grad_skip, axis=0)),
-        ("dp", "ctx"),
+    alog_total, bias_total, skip_total = load_islands(
+        (jnp.sum(grad_alog, axis=0), jnp.sum(grad_bias, axis=0), jnp.sum(grad_skip, axis=0))
     )
     return (
         grad_x.reshape(1, token_count, head_count * head_width),

time: 141 us -> 121 us (0.86)
  blocking collectives: 44.3 us -> 24 us
    psum x1 -> x2, blocking collectives: 44.3 us -> 24 us  [the longest x1 14 us: load_islands(): s_next = lax.psum(q_in, 'ctx')]
  transfers between devices with their start and end apart: 11 -> 11, of which waited for: 5 -> 5; matrix products, arithmetic and copies ran while one was open for 5% -> 7% of each run, Pallas kernels for 0% -> 0%
where the time goes in v1:
time: 121 us; the launch traced here: 120 us
  starting transfers between devices  30.8 us (25%)
  waiting for transfers between devices  26.8 us (22%)
  blocking collectives  24 us (20%)
  between operations  15.8 us (13%)
  local copies, waits for them, and re-layouts  9.75 us (8%)
  other arithmetic  8.3 us (7%)
  matrix products  4.97 us (4%)
    ppermute x10, starting transfers between devices, from_behind(): return lax.ppermute(array, axis, pairs)  30.8 us
    ppermute x10, waiting for transfers between devices, from_behind(): return lax.ppermute(array, axis, pairs)  26.8 us
    psum x1, blocking collectives, load_islands(): s_next = lax.psum(q_in, 'ctx')  14 us
    psum x1, blocking collectives, load_islands(): x_next = lax.psum(s_next, 'dp')  10 us
    unnamed x25, local copies, waits for them, and re-layouts  8.06 us
  transfers between devices with their start and end apart: 11, of which 5 were waited for; matrix products, arithmetic and copies ran while one was open for 7% of the time, Pallas kernels for 0%

profile of v1, /device:TPU:0, one launch (start us, length us, event | category | flops | bytes accessed | tf_op | source)
XLA Modules:
  0.0 120.3 jit_solution(14409676458601922094)
XLA Ops:
  7.3 0.8 reduce-window_clone.1
  8.1 1.3 %fusion.37 = (s32[]{:T(128)}, s32[4]{0:T(128)S(1)}) fusion(s32[]{:T(128)} %bitcast.18, s32[1,4]{1,0:T(1,128)S(1)} %reduce-window_clone.1, s32[1,4]{1,0:T(1,128)} %param.17), kind=kLoop, calls=%fused_computation.89 | loop fusion | flops 15 | bytes 56 | tf_op jit(solution)/shard_map/reduce_sum | solution.py:26
  13.7 1.3 %collective-permute-start = (f32[16]{0:T(128)S(1)}, f32[16]{0:T(128)S(1)}, u32[]{:S(2)}, u32[]{:S(2)}) collective-permute-start(f32[16]{0:T(128)S(1)} %get-tuple-element.105), channel_id=1, source_target_pairs={{2,0},{4,2},{6,4},{3,1},{5,3},{7,5},{10,8},{12,10},{14,12},{11,9},... | collective-permute-start | bytes 200 | tf_op jit(solution)/shard_map/ppermute | solution.py:18
  15.0 5.6 %collective-permute-start.5 = (f32[16]{0:T(128)S(1)}, f32[16]{0:T(128)S(1)}, u32[]{:S(2)}, u32[]{:S(2)}) collective-permute-start(f32[16]{0:T(128)S(1)} %get-tuple-element.105), channel_id=1, source_target_pairs={{0,2},{2,4},{4,6},{1,3},{3,5},{5,7},{8,10},{10,12},{12,14},{9,11},... | collective-permute-start | bytes 200 | tf_op jit(solution)/shard_map/ppermute | solution.py:18
  20.7 1.3 %compare_convert_fusion = (f32[128]{0:T(128)S(1)}, f32[128]{0:T(128)S(1)}) fusion(s32[128]{0:T(128)S(1)} %convert_reduce_fusion, s32[]{:T(128)} %get-tuple-element.114, s32[]{:T(128)} %bitcast.14), kind=kLoop, calls=%fused_computation.80 | loop fusion | flops 512 | bytes 1544 | tf_op jit(solution)/shard_map/vmap()/convert_element_type | solution.py:32
  23.3 1.4 %collective-permute-start.2 = (f32[16,64,128]{2,1,0:T(8,128)S(1)}, f32[16,64,128]{2,1,0:T(8,128)S(1)}, u32[]{:S(2)}, u32[]{:S(2)}) collective-permute-start(f32[16,64,128]{2,1,0:T(8,128)S(1)} %convolution_add_fusion.1), channel_id=1, source_target_pairs={{2,0},{4,2},{6,4},{3,1},{5,3},{7,5},{10,8},{12,10},{14,12},{11,9},... | collective-permute-start | bytes 1572872 | tf_op jit(solution)/shard_map/ppermute | solution.py:18
  26.0 4.6 %collective-permute-start.7 = (f32[16,64,128]{2,1,0:T(8,128)S(1)}, f32[16,64,128]{2,1,0:T(8,128)S(1)}, u32[]{:S(2)}, u32[]{:S(2)}) collective-permute-start(f32[16,64,128]{2,1,0:T(8,128)S(1)} %convolution_add_fusion), channel_id=1, source_target_pairs={{0,2},{2,4},{4,6},{1,3},{3,5},{5,7},{8,10},{10,12},{12,14},{9,11},... | collective-permute-start | bytes 1572872 | tf_op jit(solution)/shard_map/ppermute | solution.py:18
  31.6 0.9 multiply_reduce_fusion.4
  32.6 6.1 %collective-permute-done.2 = f32[16,64,128]{2,1,0:T(8,128)S(1)} collective-permute-done((f32[16,64,128]{2,1,0:T(8,128)S(1)}, f32[16,64,128]{2,1,0:T(8,128)S(1)}, u32[]{:S(2)}, u32[]{:S(2)}) %collective-permute-start.2) | collective-permute-done | bytes 524320 | tf_op jit(solution)/shard_map/ppermute | solution.py:18
  38.7 1.3 %collective-permute-start.3 = (f32[16,64,128]{2,1,0:T(8,128)S(1)}, f32[16,64,128]{2,1,0:T(8,128)}, u32[]{:S(2)}, u32[]{:S(2)}) collective-permute-start(f32[16,64,128]{2,1,0:T(8,128)S(1)} %collective-permute-done.2), channel_id=1, source_target_pairs={{2,0},{4,2},{6,4},{3,1},{5,3},{7,5},{10,8},{12,10},{14,12},{11,9},... | collective-permute-start | bytes 1572872 | tf_op jit(solution)/shard_map/ppermute | solution.py:18
  41.2 4.6 %collective-permute-start.8 = (f32[16,64,128]{2,1,0:T(8,128)S(1)}, f32[16,64,128]{2,1,0:T(8,128)S(1)}, u32[]{:S(2)}, u32[]{:S(2)}) collective-permute-start(f32[16,64,128]{2,1,0:T(8,128)S(1)} %collective-permute-done.7), channel_id=1, source_target_pairs={{0,2},{2,4},{4,6},{1,3},{3,5},{5,7},{8,10},{10,12},{12,14},{9,11},... | collective-permute-start | bytes 1572872 | tf_op jit(solution)/shard_map/ppermute | solution.py:18
  45.8 7.3 %collective-permute-done.3 = f32[16,64,128]{2,1,0:T(8,128)} collective-permute-done((f32[16,64,128]{2,1,0:T(8,128)S(1)}, f32[16,64,128]{2,1,0:T(8,128)}, u32[]{:S(2)}, u32[]{:S(2)}) %collective-permute-start.3) | collective-permute-done | bytes 524320 | tf_op jit(solution)/shard_map/ppermute | solution.py:18
  53.2 1.2 multiply_add_fusion.3
  54.3 1.3 %collective-permute-start.4 = (f32[16,64,128]{2,1,0:T(8,128)S(1)}, f32[16,64,128]{2,1,0:T(8,128)S(1)}, u32[]{:S(2)}, u32[]{:S(2)}) collective-permute-start(f32[16,64,128]{2,1,0:T(8,128)S(1)} %multiply_add_fusion.3), channel_id=1, source_target_pairs={{4,0},{6,2},{5,1},{7,3},{12,8},{14,10},{13,9},{15,11},{20,16},{22,... | collective-permute-start | bytes 1572872 | tf_op jit(solution)/shard_map/ppermute | solution.py:18
  55.8 5.5 %collective-permute-start.9 = (f32[16,64,128]{2,1,0:T(8,128)S(1)}, f32[16,64,128]{2,1,0:T(8,128)S(1)}, u32[]{:S(2)}, u32[]{:S(2)}) collective-permute-start(f32[16,64,128]{2,1,0:T(8,128)S(1)} %multiply_add_fusion.1), channel_id=1, source_target_pairs={{0,4},{2,6},{1,5},{3,7},{8,12},{10,14},{9,13},{11,15},{16,20},{18,... | collective-permute-start | bytes 1572872 | tf_op jit(solution)/shard_map/ppermute | solution.py:18
  61.5 3.9 %collective-permute-start.6 = (f32[16]{0:T(128)S(1)}, f32[16]{0:T(128)S(1)}, u32[]{:S(2)}, u32[]{:S(2)}) collective-permute-start(f32[16]{0:T(128)S(1)} %broadcast_select_fusion.1), channel_id=1, source_target_pairs={{0,2},{2,4},{4,6},{1,3},{3,5},{5,7},{8,10},{10,12},{12,14},{9,11},... | collective-permute-start | bytes 200 | tf_op jit(solution)/shard_map/ppermute | solution.py:18
  65.4 1.3 %collective-permute-start.1 = (f32[16]{0:T(128)S(1)}, f32[16]{0:T(128)S(1)}, u32[]{:S(2)}, u32[]{:S(2)}) collective-permute-start(f32[16]{0:T(128)S(1)} %broadcast_select_fusion.3), channel_id=1, source_target_pairs={{2,0},{4,2},{6,4},{3,1},{5,3},{7,5},{10,8},{12,10},{14,12},{11,9},... | collective-permute-start | bytes 200 | tf_op jit(solution)/shard_map/ppermute | solution.py:18
  66.7 3.5 %collective-permute-done.6 = f32[16]{0:T(128)S(1)} collective-permute-done((f32[16]{0:T(128)S(1)}, f32[16]{0:T(128)S(1)}, u32[]{:S(2)}, u32[]{:S(2)}) %collective-permute-start.6) | collective-permute-done | bytes 96 | tf_op jit(solution)/shard_map/ppermute | solution.py:18
  70.9 9.1 %collective-permute-done.4 = f32[16,64,128]{2,1,0:T(8,128)S(1)} collective-permute-done((f32[16,64,128]{2,1,0:T(8,128)S(1)}, f32[16,64,128]{2,1,0:T(8,128)S(1)}, u32[]{:S(2)}, u32[]{:S(2)}) %collective-permute-start.4) | collective-permute-done | bytes 524320 | tf_op jit(solution)/shard_map/ppermute | solution.py:18
  84.4 0.8 fusion.5
  85.9 14.0 %all-reduce = (f32[16]{0:T(128)S(1)}, f32[16]{0:T(128)S(1)}, f32[16]{0:T(128)S(1)}) all-reduce(f32[16]{0:T(128)S(1)} %fusion.39, f32[16]{0:T(128)S(1)} %get-tuple-element.99, f32[16]{0:T(128)S(1)} %fusion.6), channel_id=1, replica_groups=mesh['dp'=4,'ctx'=4,'head'=2] {'ctx'}, use_global_device_ids=true, to_apply=%region_19.20 | all-reduce | flops 48 | bytes 384 | tf_op jit(solution)/shard_map/psum | solution.py:10
  99.8 10.0 %all-reduce.1 = (f32[16]{0:T(128)}, f32[16]{0:T(128)}, f32[16]{0:T(128)}) all-reduce(f32[16]{0:T(128)S(1)} %get-tuple-element.91, f32[16]{0:T(128)S(1)} %get-tuple-element.92, f32[16]{0:T(128)S(1)} %get-tuple-element.93), channel_id=1, replica_groups=mesh['dp'=4,'ctx'=4,'head'=2] {'dp'}, use_global_device_ids=true, to_apply=%region_20.21 | all-reduce | flops 48 | bytes 384 | tf_op jit(solution)/shard_map/psum | solution.py:11
  110.5 0.8 copy.120
  111.4 1.5 %copy.134 = f32[1,128,128]{2,1,0:T(8,128)} copy(f32[1,128,128]{2,1,0:T(8,128)} %get-tuple-element.122) | data formatting | bytes 131072
  (87 shorter events, 15.1 us)
Async XLA Ops:
  7.2 14.8 %copy-start.2 = (bf16[1,128,1024]{2,1,0:T(8,128)(2,1)S(1)}, bf16[1,128,1024]{2,1,0:T(8,128)(2,1)}, u32[]{:S(2)}) copy-start(bf16[1,128,1024]{2,1,0:T(8,128)(2,1)} %param.16) | copy-start | bytes 786436
  7.2 104.2 %all-reduce.5.cloned.1.call-start = ((), (), s32[]{:S(2)}) async-start(), calls=%async_computation | async-start | bytes 262144 | tf_op jit(solution)/shard_map/psum | solution.py:210
  13.7 32.1 %collective-permute-start = (f32[16]{0:T(128)S(1)}, f32[16]{0:T(128)S(1)}, u32[]{:S(2)}, u32[]{:S(2)}) collective-permute-start(f32[16]{0:T(128)S(1)} %get-tuple-element.105), channel_id=1, source_target_pairs={{2,0},{4,2},{6,4},{3,1},{5,3},{7,5},{10,8},{12,10},{14,12},{11,9},... | collective-permute-start | bytes 200 | tf_op jit(solution)/shard_map/ppermute | solution.py:18
  15.0 30.8 %collective-permute-start.5 = (f32[16]{0:T(128)S(1)}, f32[16]{0:T(128)S(1)}, u32[]{:S(2)}, u32[]{:S(2)}) collective-permute-start(f32[16]{0:T(128)S(1)} %get-tuple-element.105), channel_id=1, source_target_pairs={{0,2},{2,4},{4,6},{1,3},{3,5},{5,7},{8,10},{10,12},{12,14},{9,11},... | collective-permute-start | bytes 200 | tf_op jit(solution)/shard_map/ppermute | solution.py:18
  22.3 0.8 copy-start.1
  23.0 1.7 %copy-start.6 = (f32[16]{0:T(128)S(1)}, f32[16]{0:T(128)}, u32[]{:S(2)}) copy-start(f32[16]{0:T(128)} %param.11) | copy-start | bytes 196
  23.2 1.6 %copy-start.3 = (bf16[1,128,1024]{2,1,0:T(8,128)(2,1)S(1)}, bf16[1,128,1024]{2,1,0:T(8,128)(2,1)}, u32[]{:S(2)}) copy-start(bf16[1,128,1024]{2,1,0:T(8,128)(2,1)} %param.9) | copy-start | bytes 786436
  23.3 15.4 %collective-permute-start.2 = (f32[16,64,128]{2,1,0:T(8,128)S(1)}, f32[16,64,128]{2,1,0:T(8,128)S(1)}, u32[]{:S(2)}, u32[]{:S(2)}) collective-permute-start(f32[16,64,128]{2,1,0:T(8,128)S(1)} %convolution_add_fusion.1), channel_id=1, source_target_pairs={{2,0},{4,2},{6,4},{3,1},{5,3},{7,5},{10,8},{12,10},{14,12},{11,9},... | collective-permute-start | bytes 1572872 | tf_op jit(solution)/shard_map/ppermute | solution.py:18
  25.0 0.8 copy-start
  26.0 15.2 %collective-permute-start.7 = (f32[16,64,128]{2,1,0:T(8,128)S(1)}, f32[16,64,128]{2,1,0:T(8,128)S(1)}, u32[]{:S(2)}, u32[]{:S(2)}) collective-permute-start(f32[16,64,128]{2,1,0:T(8,128)S(1)} %convolution_add_fusion), channel_id=1, source_target_pairs={{0,2},{2,4},{4,6},{1,3},{3,5},{5,7},{8,10},{10,12},{12,14},{9,11},... | collective-permute-start | bytes 1572872 | tf_op jit(solution)/shard_map/ppermute | solution.py:18
  30.7 0.7 copy-start.5
  38.7 14.5 %collective-permute-start.3 = (f32[16,64,128]{2,1,0:T(8,128)S(1)}, f32[16,64,128]{2,1,0:T(8,128)}, u32[]{:S(2)}, u32[]{:S(2)}) collective-permute-start(f32[16,64,128]{2,1,0:T(8,128)S(1)} %collective-permute-done.2), channel_id=1, source_target_pairs={{2,0},{4,2},{6,4},{3,1},{5,3},{7,5},{10,8},{12,10},{14,12},{11,9},... | collective-permute-start | bytes 1572872 | tf_op jit(solution)/shard_map/ppermute | solution.py:18
  41.2 14.4 %collective-permute-start.8 = (f32[16,64,128]{2,1,0:T(8,128)S(1)}, f32[16,64,128]{2,1,0:T(8,128)S(1)}, u32[]{:S(2)}, u32[]{:S(2)}) collective-permute-start(f32[16,64,128]{2,1,0:T(8,128)S(1)} %collective-permute-done.7), channel_id=1, source_target_pairs={{0,2},{2,4},{4,6},{1,3},{3,5},{5,7},{8,10},{10,12},{12,14},{9,11},... | collective-permute-start | bytes 1572872 | tf_op jit(solution)/shard_map/ppermute | solution.py:18
  54.3 25.7 %collective-permute-start.4 = (f32[16,64,128]{2,1,0:T(8,128)S(1)}, f32[16,64,128]{2,1,0:T(8,128)S(1)}, u32[]{:S(2)}, u32[]{:S(2)}) collective-permute-start(f32[16,64,128]{2,1,0:T(8,128)S(1)} %multiply_add_fusion.3), channel_id=1, source_target_pairs={{4,0},{6,2},{5,1},{7,3},{12,8},{14,10},{13,9},{15,11},{20,16},{22,... | collective-permute-start | bytes 1572872 | tf_op jit(solution)/shard_map/ppermute | solution.py:18
  55.8 24.3 %collective-permute-start.9 = (f32[16,64,128]{2,1,0:T(8,128)S(1)}, f32[16,64,128]{2,1,0:T(8,128)S(1)}, u32[]{:S(2)}, u32[]{:S(2)}) collective-permute-start(f32[16,64,128]{2,1,0:T(8,128)S(1)} %multiply_add_fusion.1), channel_id=1, source_target_pairs={{0,4},{2,6},{1,5},{3,7},{8,12},{10,14},{9,13},{11,15},{16,20},{18,... | collective-permute-start | bytes 1572872 | tf_op jit(solution)/shard_map/ppermute | solution.py:18
  61.5 8.7 %collective-permute-start.6 = (f32[16]{0:T(128)S(1)}, f32[16]{0:T(128)S(1)}, u32[]{:S(2)}, u32[]{:S(2)}) collective-permute-start(f32[16]{0:T(128)S(1)} %broadcast_select_fusion.1), channel_id=1, source_target_pairs={{0,2},{2,4},{4,6},{1,3},{3,5},{5,7},{8,10},{10,12},{12,14},{9,11},... | collective-permute-start | bytes 200 | tf_op jit(solution)/shard_map/ppermute | solution.py:18
  65.4 5.5 %collective-permute-start.1 = (f32[16]{0:T(128)S(1)}, f32[16]{0:T(128)S(1)}, u32[]{:S(2)}, u32[]{:S(2)}) collective-permute-start(f32[16]{0:T(128)S(1)} %broadcast_select_fusion.3), channel_id=1, source_target_pairs={{2,0},{4,2},{6,4},{3,1},{5,3},{7,5},{10,8},{12,10},{14,12},{11,9},... | collective-permute-start | bytes 200 | tf_op jit(solution)/shard_map/ppermute | solution.py:18
  82.1 0.7 copy-start.7
  85.2 0.7 copy-start.8
  111.4 1.5 %copy-start.4 = (f32[1,128,128]{2,1,0:T(8,128)S(1)}, f32[1,128,128]{2,1,0:T(8,128)}, u32[]{:S(2)}) copy-start(f32[1,128,128]{2,1,0:T(8,128)} %get-tuple-element.123) | copy-start | bytes 196612
Sparse Core Ops, SparseCore 0:
  85.3 20.8 all-reduce.4
